TPU v7x, 512 devices: a whole 4x8x8 slice. The times are simulated.
512 devices in a mesh: row: 64 (over y_hi, x, z), col: 8 (over y_lo, core).
Axes of the slice: x: 4, y: 8 (y_hi: 2, y_lo: 4; y = y_hi * 4 + y_lo), z: 8, core: 2. Of those that a mesh axis runs over, the one named last changes fastest.
Arguments:
- features: bfloat16 [65536, 1024], P(('row', 'col')), may hold values from -6 to 6
- history: bfloat16 [65536, 1024], P(('row', 'col')), may hold values from -6 to 6
- degree: int32 [65536], P(('row', 'col')), may hold values from 8 to 64
- adj_tiles: bfloat16 [3072, 128, 128], P(('row', 'col')), may hold values from 0 to 3, as said below
- tile_index: int32 [3072], P(('row', 'col')), may hold values from 0 to 23, as said below
- tile_count: int32 [512], P(('row', 'col')), may hold values from 3 to 6, as said below
- weight: bfloat16 [1024, 1024], P(None, 'col'), may hold values from -0.1875 to 0.1875
- cotangent: bfloat16 [65536, 1024], P(('row', 'col')), may hold values from -6 to 6
Outputs:
- layer_out: bfloat16 [65536, 1024], P(('row', 'col'))
- grad_features: bfloat16 [65536, 1024], P(('row', 'col'))
- grad_weight: float32 [1024, 1024], P(None, 'col')
Inputs may be any that keep to these rules, and one draw needn't show every extreme that they name: `adj_tiles`: whole numbers: the edge counts of a tile's entries. Slots from tile_count on of a device are never read. `tile_index`: the codes of one device's 6 slots are distinct. Its first three slots hold tiles whose column block lies in the first, the last and the middle third of the 3 m column blocks, in that order. `tile_count`: some device has 6 live slots in every draw.
All inputs are finite; a program needn't handle non-finite values.
Results may differ from a plain program's by a relative error of at most 0.014.
Values may be sent and summed in bfloat16 or wider, within the bound.
No kernel may reach another device: no remote copies, remote signals or barrier semaphores. Data moves between devices by JAX's collectives and lax.ppermute only.
A program may use at most 64 MiB of HBM per device.

v0:
```python
import math
import jax
import jax.numpy as jnp
from jax import lax
from jax.sharding import PartitionSpec as P

TILE = 128


def padded_2(x, sides, width):
    for axis, dim in sides:
        count, length = (lax.axis_size(axis), x.shape[dim])
        up = [(i, (i + 1) % count) for i in range(count - 1)]
        down = [(j, i) for i, j in up]
        last = lax.slice_in_dim(x, length - width, length, axis=dim)
        initial = lax.slice_in_dim(x, 0, width, axis=dim)
        before = lax.ppermute(last, axis, up)
        after = lax.ppermute(initial, axis, down)
        x = jnp.concatenate([before, x, after], axis=dim)
    return x


def inverse_root(degree):
    return 1.0 / jnp.sqrt(degree.astype(jnp.float32))


def silu_slope(pre_act):
    sigmoid = jax.nn.sigmoid(pre_act)
    return sigmoid * (1.0 + pre_act * (1.0 - sigmoid))


def per_device(features, history, degree, adj_tiles, tile_index, tile_count, weight, cotangent):
    slab_rows = features.shape[0]
    col_count = lax.axis_size("col")
    blocks = slab_rows // TILE
    src_width = 3 * blocks
    part_rows = slab_rows * col_count
    own_scale = inverse_root(degree)
    own_src = (features.astype(jnp.float32) * own_scale[:, None]).astype(jnp.bfloat16)
    hist_src = (history.astype(jnp.float32) * own_scale[:, None]).astype(jnp.bfloat16)
    padded = padded_2(hist_src, (("row", 0),), slab_rows)
    sources = jnp.concatenate([padded[:slab_rows], own_src, padded[2 * slab_rows :]], axis=0)
    live_tiles = tile_count[0]

    def add_tile(slot_at, summed):
        tile_code = tile_index[slot_at]
        dest_block = tile_code // src_width
        src_block = tile_code % src_width
        source_rows = lax.dynamic_slice_in_dim(sources, src_block * TILE, TILE, 0)
        product = jnp.dot(adj_tiles[slot_at], source_rows, preferred_element_type=jnp.float32)
        current = lax.dynamic_slice_in_dim(summed, dest_block * TILE, TILE, 0)
        return lax.dynamic_update_slice_in_dim(summed, current + product, dest_block * TILE, 0)

    partial_sum = lax.fori_loop(
        0, live_tiles, add_tile, jnp.zeros((part_rows, features.shape[1]), jnp.float32)
    )
    aggregate_raw = lax.psum_scatter(
        partial_sum.astype(jnp.bfloat16), "col", scatter_dimension=0, tiled=True
    ).astype(jnp.float32)
    aggregated = (aggregate_raw * own_scale[:, None]).astype(jnp.bfloat16)
    whole_weight = lax.all_gather(weight, "col", axis=1, tiled=True)
    pre_act = jnp.dot(aggregated, whole_weight, preferred_element_type=jnp.float32)
    layer_out = jax.nn.silu(pre_act).astype(jnp.bfloat16)
    grad_pre = (cotangent.astype(jnp.float32) * silu_slope(pre_act)).astype(jnp.bfloat16)
    back_prop = lax.dot_general(
        grad_pre, whole_weight, (((1,), (1,)), ((), ())), preferred_element_type=jnp.float32
    )
    dest_grad = (back_prop * own_scale[:, None]).astype(jnp.bfloat16)
    all_dest = lax.all_gather(dest_grad, "col", axis=0, tiled=True)

    def add_grad(slot_at, summed):
        tile_code = tile_index[slot_at]
        dest_block = tile_code // src_width
        src_block = tile_code % src_width - blocks
        inside = (src_block >= 0) & (src_block < blocks)

        def accumulate(running):
            dest_rows = lax.dynamic_slice_in_dim(all_dest, dest_block * TILE, TILE, 0)
            product = lax.dot_general(
                adj_tiles[slot_at],
                dest_rows,
                (((0,), (0,)), ((), ())),
                preferred_element_type=jnp.float32,
            )
            return running + product

        def unchanged(running):
            return running

        return lax.cond(inside, accumulate, unchanged, summed)

    grad_sum = lax.fori_loop(0, live_tiles, add_grad, jnp.zeros(features.shape, jnp.float32))
    grad_features = (grad_sum * own_scale[:, None]).astype(jnp.bfloat16)
    node_total = part_rows * lax.axis_size("row")
    loss_scale = 1.0 / math.sqrt(node_total)
    out_cols = weight.shape[1]
    local_term = lax.dot_general(
        aggregated, grad_pre, (((0,), (0,)), ((), ())), preferred_element_type=jnp.float32
    )
    summed_all = lax.psum(local_term, ("row", "col"))
    grad_weight = (
        lax.dynamic_slice_in_dim(summed_all, lax.axis_index("col") * out_cols, out_cols, 1)
        * loss_scale
    )
    return (layer_out, grad_features, grad_weight)


def solution(mesh):
    in_specs = (
        P(("row", "col"), None),
        P(("row", "col"), None),
        P(("row", "col")),
        P(("row", "col"), None, None),
        P(("row", "col")),
        P(("row", "col")),
        P(None, "col"),
        P(("row", "col"), None),
    )
    out_specs = (P(("row", "col"), None), P(("row", "col"), None), P(None, "col"))
    return jax.shard_map(
        per_device, mesh=mesh, in_specs=in_specs, out_specs=out_specs, check_vma=False
    )
```

profile of v0, /device:TPU:135, one launch (start us, length us, event | category | flops | bytes accessed | tf_op | source)
XLA Modules:
  0.0 481.6 jit_solution(10469675945475615984)
XLA Ops:
  7.2 0.0 all-gather.3.cloned.1.call-start
  7.2 0.7 all-gather.3.cloned.1.call-update
  7.9 0.0 reduce-scatter.2.cloned.1.call-start
  7.9 0.7 convert_rsqrt_fusion
  8.6 1.2 multiply_convert_fusion.4
  9.8 4.0 collective-permute-start
  13.8 1.9 collective-permute-start.1
  15.7 3.1 collective-permute-done
  18.9 5.9 %collective-permute-done.1 = bf16[128,1024]{1,0:T(8,128)(2,1)S(1)} collective-permute-done((bf16[128,1024]{1,0:T(8,128)(2,1)S(1)}, bf16[128,1024]{1,0:T(8,128)(2,1)S(1)}, u32[]{:S(2)}, u32[]{:S(2)}) %collective-permute-start.1) | collective-permute-done | bytes 262176 | tf_op jit(solution)/shard_map/ppermute | solution.py:18
  24.7 0.1 pad_maximum_fusion
  24.8 0.0 copy-start.3
  24.8 2.5 broadcast_in_dim.4
  27.3 0.0 copy-done.3
  27.3 32.6 %while.28 = (s32[]{:T(128)}, f32[1024,1024]{1,0:T(8,128)}, s32[]{:T(128)}, s32[6]{0:T(128)S(1)}, bf16[6,128,128]{2,1,0:T(8,128)(2,1)}, /*index=5*/bf16[384,1024]...) while((s32[]{:T(128)}, f32[1024,1024]{1,0:T(8,128)}, ...), condition=%wide.region_1.2_spmd, body=%wide.region_0.1_spmd.sunk | while | flops 33685528 | bytes 1343902 | solution.py:54
  28.0 0.6 dynamic_slice.63
  30.5 2.1 fusion.19
  33.3 0.6 dynamic_slice.63
  35.8 2.1 fusion.19
  38.6 0.6 dynamic_slice.63
  41.2 2.1 fusion.19
  43.9 0.6 dynamic_slice.63
  46.5 2.1 fusion.19
  49.3 0.6 dynamic_slice.63
  51.8 2.1 fusion.19
  54.6 0.6 dynamic_slice.63
  57.2 2.1 fusion.19
  59.9 3.9 convert_element_type.51
  63.8 0.0 reduce-scatter.2.cloned.1.call-update
  63.8 0.0 copy-start
  63.8 0.0 all-reduce.2.cloned.1.call-start
  63.9 0.0 all-gather.3.cloned.1.call-done
  63.9 51.4 %reduce-scatter.2.cloned.1.call-done = bf16[128,1024]{1,0:T(8,128)(2,1)} async-done(((bf16[1024,1024]{1,0:T(8,128)(2,1)}), bf16[128,1024]{1,0:T(8,128)(2,1)}) %reduce-scatter.2.cloned.1.call-update) | async-done | bytes 262160 | tf_op jit(solution)/shard_map/reduce_scatter | solution.py:57
  115.3 0.0 copy-start.1
  115.3 3.0 multiply_convert_fusion.2
  118.3 0.0 copy-done
  118.3 0.0 copy-done.1
  118.3 2.8 fusion.10
  121.2 0.0 copy-start.2
  121.2 0.0 all-reduce.2.cloned.1.call-update
  121.2 0.0 all-gather.5.cloned.1.call-start
  121.2 1.5 copy-done.2
  122.8 1.6 fusion.9
  124.3 0.0 all-gather.5.cloned.1.call-update
  124.3 285.7 %all-reduce.2.cloned.1.call-done = f32[1024,1024]{1,0:T(8,128)} async-done(((f32[1024,1024]{1,0:T(8,128)}), f32[1024,1024]{1,0:T(8,128)}) %all-reduce.2.cloned.1.call-update) | async-done | bytes 4194320 | tf_op jit(solution)/shard_map/psum | solution.py:100
  410.0 1.9 dynamic-slice_multiply_fusion
  411.9 37.2 %all-gather.5.cloned.1.call-done = bf16[1024,1024]{1,0:T(8,128)(2,1)} async-done(((bf16[128,1024]{1,0:T(8,128)(2,1)}), bf16[1024,1024]{1,0:T(8,128)(2,1)}) %all-gather.5.cloned.1.call-update) | async-done | bytes 2097168 | tf_op jit(solution)/shard_map/all_gather | solution.py:69
  449.1 25.2 %while.29 = (s32[]{:T(128)}, f32[128,1024]{1,0:T(8,128)S(1)}, s32[]{:T(128)}, s32[6]{0:T(128)S(1)}, bf16[6,128,128]{2,1,0:T(8,128)(2,1)}, /*index=5*/bf16[1024,1...) while((s32[]{:T(128)}, f32[128,1024]{1,0:T(8,128)S(1)}, s32[]{:T(128)}, ...), condition=%wide.region_6.7_spmd, body=%wide.region_3.6_spmd.sunk | while | flops 33685536 | bytes 1343953 | solution.py:92
  449.8 0.6 dynamic_slice.64
  451.7 0.6 dynamic_slice.64
  453.7 0.6 dynamic_slice.64
  454.9 3.2 conditional.2
  456.9 1.2 convolution_add_fusion.1
  458.8 0.6 dynamic_slice.64
  460.1 3.2 conditional.2
  462.1 1.2 convolution_add_fusion.1
  464.0 0.6 dynamic_slice.64
  465.2 3.2 conditional.2
  467.2 1.2 convolution_add_fusion.1
  469.1 0.6 dynamic_slice.64
  470.4 3.2 conditional.2
  472.4 1.2 convolution_add_fusion.1
  474.3 0.8 multiply_convert_fusion
  (3 shorter events, 0.1 us)
Async XLA Ops:
  7.2 56.7 %all-gather.3.cloned.1.call-start = ((), (), s32[]{:S(2)}) async-start(), calls=%async_computation.2 | async-start | bytes 2359296 | tf_op jit(solution)/shard_map/all_gather | solution.py:61
  7.9 107.4 %reduce-scatter.2.cloned.1.call-start = ((), (), s32[]{:S(2)}) async-start(), calls=%async_computation.1 | async-start | bytes 2359296 | tf_op jit(solution)/shard_map/reduce_scatter | solution.py:57
  9.8 9.1 %collective-permute-start = (bf16[128,1024]{1,0:T(8,128)(2,1)S(1)}, bf16[128,1024]{1,0:T(8,128)(2,1)S(1)}, u32[]{:S(2)}, u32[]{:S(2)}) collective-permute-start(bf16[128,1024]{1,0:T(8,128)(2,1)S(1)} %get-tuple-element.260), channel_id=1, source_target_pairs={{0,8},{8,16},{16,24},{24,32},{32,40},{40,48},{48,56},{56,64},{64,7... | collective-permute-start | bytes 786440 | tf_op jit(solution)/shard_map/ppermute | solution.py:17
  13.8 10.9 %collective-permute-start.1 = (bf16[128,1024]{1,0:T(8,128)(2,1)S(1)}, bf16[128,1024]{1,0:T(8,128)(2,1)S(1)}, u32[]{:S(2)}, u32[]{:S(2)}) collective-permute-start(bf16[128,1024]{1,0:T(8,128)(2,1)S(1)} %get-tuple-element.260), channel_id=1, source_target_pairs={{8,0},{16,8},{24,16},{32,24},{40,32},{48,40},{56,48},{64,56},{72,6... | collective-permute-start | bytes 786440 | tf_op jit(solution)/shard_map/ppermute | solution.py:18
  24.8 2.5 copy-start.3
  63.8 54.5 %copy-start = (bf16[128,1024]{1,0:T(8,128)(2,1)S(1)}, bf16[128,1024]{1,0:T(8,128)(2,1)}, u32[]{:S(2)}) copy-start(bf16[128,1024]{1,0:T(8,128)(2,1)} %param.21) | copy-start | bytes 786436
  63.8 346.2 %all-reduce.2.cloned.1.call-start = ((), (), s32[]{:S(2)}) async-start(), calls=%async_computation.4 | async-start | bytes 8388608 | tf_op jit(solution)/shard_map/psum | solution.py:100
  115.3 3.0 copy-start.1
  121.2 1.6 copy-start.2
  121.2 327.9 %all-gather.5.cloned.1.call-start = ((), (), s32[]{:S(2)}) async-start(), calls=%async_computation.3 | async-start | bytes 2359296 | tf_op jit(solution)/shard_map/all_gather | solution.py:69
Sparse Core Ops, SparseCore 0:
  10.0 44.7 all-gather.2
  63.9 51.3 reduce-scatter.1
  121.3 288.6 all-reduce.1
  412.5 36.5 all-gather.4
where the time goes:
time: 483 us; the launch traced here: 482 us
  waiting for transfers between devices  384 us (80%)
  loops' own time  33.2 us (7%)
  matrix products  24.9 us (5%)
  between operations  13.8 us (3%)
  local copies, waits for them, and re-layouts  11.1 us (2%)
  other arithmetic  8.45 us (2%)
  starting transfers between devices  6.08 us (1%)
    psum x1, waiting for transfers between devices, per_device(): summed_all = lax.psum(local_term, ('row', 'col'))  286 us
    reduce_scatter x1, waiting for transfers between devices, per_device(): lax.psum_scatter(partial_sum.astype(jnp.bfloat16), 'col', scatter_dimensi...  51.4 us
    all_gather x1, waiting for transfers between devices, per_device(): all_dest = lax.all_gather(dest_grad, 'col', axis=0, tiled=True)  37.2 us
    another operation x1, loops' own time, per_device(): lax.fori_loop(0, live_tiles, add_tile, jnp.zeros((part_rows, features.sha...  16.5 us
    dot_general x6, matrix products, add_tile(): jnp.dot(adj_tiles[slot_at], source_rows, preferred_element_type=jnp.float32)  12.6 us
  transfers between devices with their start and end apart: 6, of which 5 were waited for; matrix products, arithmetic and copies ran while one was open for 6% of the time, Pallas kernels for 0%

commit v1 on v0

--- a/solution.py
+++ b/solution.py
@@ -97,7 +97,8 @@
     local_term = lax.dot_general(
         aggregated, grad_pre, (((0,), (0,)), ((), ())), preferred_element_type=jnp.float32
     )
-    summed_all = lax.psum(local_term, ("row", "col"))
+    inner = lax.psum(local_term, "col")
+    summed_all = lax.psum(inner, "row")
     grad_weight = (
         lax.dynamic_slice_in_dim(summed_all, lax.axis_index("col") * out_cols, out_cols, 1)
         * loss_scale

time: 483 us -> 1150 us (2.38)
  the two profiles are of different devices: /device:TPU:135 before, /device:TPU:8 now
where the time goes in v1:
time: 1150 us
  waiting for transfers between devices  1070 us (93%)
  loops' own time  25.3 us (2%)
  matrix products  20.3 us (2%)
  between operations  13.8 us (1%)
    psum x1, waiting for transfers between devices, per_device(): summed_all = lax.psum(inner, 'row')  848 us
    psum x1, waiting for transfers between devices, per_device(): inner = lax.psum(local_term, 'col')  111 us
    reduce_scatter x1, waiting for transfers between devices, per_device(): lax.psum_scatter(partial_sum.astype(jnp.bfloat16), 'col', scatter_dimensi...  56 us
    all_gather x1, waiting for transfers between devices, per_device(): all_dest = lax.all_gather(dest_grad, 'col', axis=0, tiled=True)  43 us
  transfers between devices with their start and end apart: 7, of which 7 were waited for; matrix products, arithmetic and copies ran while one was open for 3% of the time, Pallas kernels for 0%

profile of v1, /device:TPU:8, one launch (start us, length us, event | category | flops | bytes accessed | tf_op | source)
XLA Modules:
  0.0 1152.7 jit_solution(13738026002796385310)
XLA Ops:
  7.2 0.0 all-gather.3.cloned.1.call-start
  7.2 0.7 all-gather.3.cloned.1.call-update
  7.9 0.0 reduce-scatter.2.cloned.1.call-start
  7.9 0.7 convert_rsqrt_fusion
  8.6 1.2 multiply_convert_fusion.4
  9.8 4.3 collective-permute-start
  14.1 1.3 collective-permute-start.1
  15.4 4.2 collective-permute-done
  19.6 4.8 collective-permute-done.1
  24.4 0.1 pad_maximum_fusion
  24.4 0.0 copy-start.3
  24.4 2.5 broadcast_in_dim.4
  26.9 0.0 copy-done.3
  26.9 27.3 %while.28 = (s32[]{:T(128)}, f32[1024,1024]{1,0:T(8,128)}, s32[]{:T(128)}, s32[6]{0:T(128)S(1)}, bf16[6,128,128]{2,1,0:T(8,128)(2,1)}, /*index=5*/bf16[384,1024]...) while((s32[]{:T(128)}, f32[1024,1024]{1,0:T(8,128)}, ...), condition=%wide.region_1.2_spmd, body=%wide.region_0.1_spmd.sunk | while | flops 33685528 | bytes 1343902 | solution.py:54
  27.6 0.6 dynamic_slice.63
  30.2 2.1 fusion.19
  32.9 0.6 dynamic_slice.63
  35.5 2.1 fusion.19
  38.3 0.6 dynamic_slice.63
  40.8 2.1 fusion.19
  43.6 0.6 dynamic_slice.63
  46.2 2.1 fusion.19
  48.9 0.6 dynamic_slice.63
  51.5 2.1 fusion.19
  54.3 3.9 convert_element_type.51
  58.2 0.0 reduce-scatter.2.cloned.1.call-update
  58.2 0.0 copy-start
  58.2 0.0 all-reduce.3.cloned.1.call-start
  58.3 1.9 all-gather.3.cloned.1.call-done
  60.2 56.0 %reduce-scatter.2.cloned.1.call-done = bf16[128,1024]{1,0:T(8,128)(2,1)} async-done(((bf16[1024,1024]{1,0:T(8,128)(2,1)}), bf16[128,1024]{1,0:T(8,128)(2,1)}) %reduce-scatter.2.cloned.1.call-update) | async-done | bytes 262160 | tf_op jit(solution)/shard_map/reduce_scatter | solution.py:57
  116.1 0.0 copy-start.1
  116.1 3.0 multiply_convert_fusion.2
  119.1 0.0 copy-done
  119.1 0.0 copy-done.1
  119.1 2.9 fusion.10
  122.0 0.0 copy-start.2
  122.0 0.0 all-reduce.3.cloned.1.call-update
  122.0 0.0 all-gather.5.cloned.1.call-start
  122.0 1.5 copy-done.2
  123.5 1.6 fusion.9
  125.1 0.0 all-gather.5.cloned.1.call-update
  125.1 0.0 all-reduce.5.cloned.1.call-start
  125.2 110.5 %all-reduce.3.cloned.1.call-done = f32[1024,1024]{1,0:T(8,128)} async-done(((f32[1024,1024]{1,0:T(8,128)}), f32[1024,1024]{1,0:T(8,128)}) %all-reduce.3.cloned.1.call-update) | async-done | bytes 4194320 | tf_op jit(solution)/shard_map/psum | solution.py:100
  235.7 0.0 all-reduce.5.cloned.1.call-update
  235.7 43.0 %all-gather.5.cloned.1.call-done = bf16[1024,1024]{1,0:T(8,128)(2,1)} async-done(((bf16[128,1024]{1,0:T(8,128)(2,1)}), bf16[1024,1024]{1,0:T(8,128)(2,1)}) %all-gather.5.cloned.1.call-update) | async-done | bytes 2097168 | tf_op jit(solution)/shard_map/all_gather | solution.py:69
  278.8 16.8 %while.29 = (s32[]{:T(128)}, f32[128,1024]{1,0:T(8,128)S(1)}, s32[]{:T(128)}, s32[6]{0:T(128)S(1)}, bf16[6,128,128]{2,1,0:T(8,128)(2,1)}, /*index=5*/bf16[1024,1...) while((s32[]{:T(128)}, f32[128,1024]{1,0:T(8,128)S(1)}, s32[]{:T(128)}, ...), condition=%wide.region_6.7_spmd, body=%wide.region_3.6_spmd.sunk | while | flops 33685536 | bytes 1343953 | solution.py:92
  279.4 0.6 dynamic_slice.64
  281.4 0.6 dynamic_slice.64
  283.3 0.6 dynamic_slice.64
  284.6 3.2 conditional.2
  286.6 1.2 convolution_add_fusion.1
  288.5 0.6 dynamic_slice.64
  290.4 0.6 dynamic_slice.64
  291.7 3.2 conditional.2
  293.7 1.2 convolution_add_fusion.1
  295.5 0.8 multiply_convert_fusion
  296.3 847.9 %all-reduce.5.cloned.1.call-done = f32[1024,1024]{1,0:T(8,128)} async-done(((f32[1024,1024]{1,0:T(8,128)}), f32[1024,1024]{1,0:T(8,128)}) %all-reduce.5.cloned.1.call-update) | async-done | bytes 4194320 | tf_op jit(solution)/shard_map/psum | solution.py:101
  1144.3 1.9 dynamic-slice_multiply_fusion
  (4 shorter events, 0.1 us)
Async XLA Ops:
  7.2 53.0 %all-gather.3.cloned.1.call-start = ((), (), s32[]{:S(2)}) async-start(), calls=%async_computation.2 | async-start | bytes 2359296 | tf_op jit(solution)/shard_map/all_gather | solution.py:61
  7.9 108.2 %reduce-scatter.2.cloned.1.call-start = ((), (), s32[]{:S(2)}) async-start(), calls=%async_computation.1 | async-start | bytes 2359296 | tf_op jit(solution)/shard_map/reduce_scatter | solution.py:57
  9.8 9.8 collective-permute-start
  14.1 10.3 collective-permute-start.1
  24.4 2.5 copy-start.3
  58.2 60.9 %copy-start = (bf16[128,1024]{1,0:T(8,128)(2,1)S(1)}, bf16[128,1024]{1,0:T(8,128)(2,1)}, u32[]{:S(2)}) copy-start(bf16[128,1024]{1,0:T(8,128)(2,1)} %param.21) | copy-start | bytes 786436
  58.2 177.5 %all-reduce.3.cloned.1.call-start = ((), (), s32[]{:S(2)}) async-start(), calls=%async_computation.4 | async-start | bytes 8388608 | tf_op jit(solution)/shard_map/psum | solution.py:100
  116.1 3.0 copy-start.1
  122.0 1.6 copy-start.2
  122.0 156.7 %all-gather.5.cloned.1.call-start = ((), (), s32[]{:S(2)}) async-start(), calls=%async_computation.3 | async-start | bytes 2359296 | tf_op jit(solution)/shard_map/all_gather | solution.py:69
  125.1 1019.1 %all-reduce.5.cloned.1.call-start = ((), (), s32[]{:S(2)}) async-start(), calls=%async_computation.5 | async-start | bytes 8388608 | tf_op jit(solution)/shard_map/psum | solution.py:101
Sparse Core Ops, SparseCore 0:
  10.0 50.1 all-gather.2
  63.0 53.0 reduce-scatter.1
  122.1 113.5 all-reduce.2
  238.2 40.4 all-gather.4
  281.5 862.7 all-reduce.4
